TPU v7x, 32 devices: a whole 2x2x4 slice. The times are simulated.
32 devices in a mesh: row: 4 (over y, core), col: 8 (over z, x).
Axes of the slice: x: 2, y: 2, z: 4, core: 2. Of those that a mesh axis runs over, the one named last changes fastest.
Arguments:
- left: bfloat16 [128, 8192], P('col', 'row'), may hold values from -6 to 6
- right: bfloat16 [128, 8192], P('row', 'col'), may hold values from -6 to 6
- proj: bfloat16 [1024, 128], replicated, may hold values from -2 to 2
- bias: float32 [128], replicated, may hold values from -1 to 1
- pair_grad: bfloat16 [256, 256, 128], P('row', 'col'), may hold values from -0.1875 to 0.1875
Outputs:
- pair_out: bfloat16 [256, 256, 128], P('row', 'col')
- left_grad: float32 [128, 8192], P('col', 'row')
- right_grad: float32 [128, 8192], P('row', 'col')
- proj_grad: float32 [1024, 128], replicated
All inputs are finite; a program needn't handle non-finite values.
Results may differ from a plain program's by a relative error of at most 0.0056.
Values may be sent and summed in bfloat16 or wider, within the bound.
A program may use at most 128 MiB of HBM per device.

v0:
```python
import jax
import jax.numpy as jnp
from jax import lax
from jax.sharding import PartitionSpec as P

CH = 32
PAIR = 128
SEQS = 128
OUTER = 1024


def shards(left, right, proj, bias, pair_grad):
    left_all = lax.all_gather(left, "col", axis=0, tiled=True)
    right_all = lax.all_gather(right, "row", axis=0, tiled=True)
    seq_count = left_all.shape[0]
    rows_here = left_all.shape[1] // CH
    cols_here = right_all.shape[1] // CH
    left_cube = left_all.reshape(seq_count, rows_here, CH)
    right_cube = right_all.reshape(seq_count, cols_here, CH)
    square = (
        jnp.einsum("sic,sje->ijce", left_cube, right_cube, preferred_element_type=jnp.float32)
        / SEQS
    )
    outers = square.astype(jnp.bfloat16).reshape(rows_here * cols_here, OUTER)
    preact = jnp.dot(outers, proj, preferred_element_type=jnp.float32) + bias
    active = jnp.maximum(preact, 0.0)
    pair_out = (active * active).astype(jnp.bfloat16).reshape(rows_here, cols_here, PAIR)
    grad_pre = (
        pair_grad.reshape(rows_here * cols_here, PAIR).astype(jnp.float32) * 2.0 * active
    ).astype(jnp.bfloat16)
    weight_term = lax.dot_general(
        outers, grad_pre, (((0,), (0,)), ((), ())), preferred_element_type=jnp.float32
    )
    proj_grad = lax.psum(weight_term, ("row", "col"))
    grad_outer = jnp.dot(grad_pre, proj.T, preferred_element_type=jnp.float32).astype(jnp.bfloat16)
    grad_cube = grad_outer.reshape(rows_here, cols_here, CH, CH)
    left_whole = (
        jnp.einsum("ijce,sje->sic", grad_cube, right_cube, preferred_element_type=jnp.float32)
        / SEQS
    )
    right_whole = (
        jnp.einsum("ijce,sic->sje", grad_cube, left_cube, preferred_element_type=jnp.float32) / SEQS
    )
    left_grad = lax.psum_scatter(
        left_whole.reshape(seq_count, rows_here * CH), "col", scatter_dimension=0, tiled=True
    )
    right_grad = lax.psum_scatter(
        right_whole.reshape(seq_count, cols_here * CH), "row", scatter_dimension=0, tiled=True
    )
    return (pair_out, left_grad, right_grad, proj_grad)


def solution(mesh):
    return jax.shard_map(
        shards,
        mesh=mesh,
        in_specs=(P("col", "row"), P("row", "col"), P(), P(), P("row", "col", None)),
        out_specs=(P("row", "col", None), P("col", "row"), P("row", "col"), P()),
        check_vma=False,
    )
```

profile of v0, /device:TPU:0, one launch (start us, length us, event | category | flops | bytes accessed | tf_op | source)
XLA Modules:
  0.0 248.4 jit_solution(3948851120335303654)
XLA Ops:
  8.0 0.0 copy-start
  8.0 0.0 all-reduce.2.cloned.1.call-start
  8.1 33.4 %all_gather.7 = bf16[128,2048]{1,0:T(8,128)(2,1)S(1)} all-gather(bf16[16,2048]{1,0:T(8,128)(2,1)} %param.5), channel_id=1, replica_groups=mesh['row'=4,'col'=8] {'col'}, dimensions={0}, use_global_device_ids=true | all-gather | bytes 589824 | tf_op jit(solution)/shard_map/all_gather | solution.py:13
  41.4 0.3 copy.26
  41.7 6.0 %all_gather.6 = bf16[128,1024]{1,0:T(8,128)(2,1)S(1)} all-gather(bf16[32,1024]{1,0:T(8,128)(2,1)} %param.6), channel_id=1, replica_groups=mesh['row'=4,'col'=8] {'row'}, dimensions={0}, use_global_device_ids=true | all-gather | bytes 327680 | tf_op jit(solution)/shard_map/all_gather | solution.py:14
  47.7 0.2 copy.25
  47.9 5.6 %fusion = bf16[64,32,32,32]{0,3,2,1:T(8,128)(2,1)} fusion(bf16[128,32,32,1]{0,2,3,1:T(8,128)(2,1)S(1)} %bitcast.50, bf16[128,64,32]{0,2,1:T(8,128)(2,1)S(1)} %bitcast.48), kind=kOutput, calls=%fused_computation.1 | convolution fusion | flops 541065216 | bytes 4980736 | tf_op jit(solution)/shard_map/sic,sje->ijce/dot_general | solution.py:21
  53.5 24.6 %copy.28 = bf16[64,32,32,32]{3,2,1,0:T(8,128)(2,1)} copy(bf16[64,32,32,32]{0,3,2,1:T(8,128)(2,1)} %fusion) | data formatting | bytes 8388608 | tf_op jit(solution)/shard_map/convert_element_type | solution.py:24
  78.1 0.0 copy-start.2
  78.1 0.0 copy-start.3
  78.1 23.3 %reshape.36 = bf16[2048,1024]{1,0:T(8,128)(2,1)} reshape(bf16[64,32,32,32]{3,2,1,0:T(8,128)(2,1)} %copy.28) | data formatting | bytes 8388608 | tf_op jit(solution)/shard_map/reshape | solution.py:24
  101.4 0.0 copy-done.2
  101.4 0.0 copy-start.1
  101.4 0.1 convert_multiply_fusion
  101.6 0.0 copy-done
  101.6 0.0 copy-done.3
  101.6 4.4 %fusion.4 = (bf16[2048,128]{1,0:T(8,128)(2,1)S(1)}, bf16[2048,128]{1,0:T(8,128)(2,1)}) fusion(f32[64,32,128]{2,1,0:T(8,128)S(1)} %convert_multiply_fusion, f32[128]{0:T(128)S(1)} %copy-done.3, bf16[2048,1024]{1,0:T(8,128)(2,1)} %reshape.36, bf16[1024,128]{1,0:T(8,128)(2,1)S(1)} %copy-done), kind=kOutput, calls=%fused_computation.10 | convolution fusion | flops 538443776 | bytes 6554112 | tf_op jit(solution)/shard_map/dot_general | solution.py:25
  106.0 0.0 copy-done.1
  106.0 2.1 fusion.7
  108.1 0.0 all-reduce.2.cloned.1.call-update
  108.1 0.2 reduce-scatter.5.cloned.1.call-start
  108.3 3.2 %convolution_convert_fusion = bf16[2048,1024]{1,0:T(8,128)(2,1)} fusion(bf16[2048,128]{1,0:T(8,128)(2,1)S(1)} %get-tuple-element.4, bf16[1024,128]{1,0:T(8,128)(2,1)S(1)} %copy-done), kind=kOutput, calls=%fused_computation.2 | convolution fusion | flops 538968064 | bytes 4980736 | tf_op jit(solution)/shard_map/dot_general | solution.py:35
  111.5 20.3 %reshape.38 = bf16[64,32,32,32]{3,2,1,0:T(8,128)(2,1)} reshape(bf16[2048,1024]{1,0:T(8,128)(2,1)} %convolution_convert_fusion) | data formatting | bytes 8388608 | tf_op jit(solution)/shard_map/reshape | solution.py:36
  131.9 10.3 %fusion.3 = f32[32,32,128]{2,1,0:T(8,128)S(1)} fusion(bf16[64,32,32,32]{3,2,1,0:T(8,128)(2,1)} %reshape.38, bf16[128,64,32,1]{0,2,3,1:T(8,128)(2,1)S(1)} %bitcast.49), kind=kOutput, calls=%fused_computation.8 | convolution fusion | flops 537001984 | bytes 5242880 | tf_op jit(solution)/shard_map/ijce,sic->sje/dot_general | solution.py:42
  142.2 1.0 copy.31
  143.2 0.0 reduce-scatter.5.cloned.1.call-update
  143.2 0.0 reduce-scatter.3.cloned.1.call-start
  143.3 9.1 %fusion.2 = f32[64,32,128]{2,1,0:T(8,128)S(1)} fusion(bf16[64,32,32,32]{3,2,1,0:T(8,128)(2,1)} %reshape.38, bf16[128,32,32,1]{0,2,1,3:T(8,128)(2,1)S(1)} %bitcast.51), kind=kOutput, calls=%fused_computation.6 | convolution fusion | flops 537133056 | bytes 5505024 | tf_op jit(solution)/shard_map/ijce,sje->sic/dot_general | solution.py:38
  152.4 1.3 copy.29
  153.7 0.0 reduce-scatter.3.cloned.1.call-update
  153.8 85.4 %all-reduce.2.cloned.1.call-done = f32[1024,128]{1,0:T(8,128)} async-done(((f32[1024,128]{1,0:T(8,128)}), f32[1024,128]{1,0:T(8,128)}) %all-reduce.2.cloned.1.call-update) | async-done | bytes 524304 | tf_op jit(solution)/shard_map/psum | solution.py:34
  239.1 0.0 reduce-scatter.5.cloned.1.call-done
  239.1 0.0 reduce-scatter.3.cloned.1.call-done
  239.1 1.9 copy.41
Async XLA Ops:
  8.0 93.6 %copy-start = (bf16[1024,128]{1,0:T(8,128)(2,1)S(1)}, bf16[1024,128]{1,0:T(8,128)(2,1)}, u32[]{:S(2)}) copy-start(bf16[1024,128]{1,0:T(8,128)(2,1)} %param.7) | copy-start | bytes 786436
  8.0 231.1 %all-reduce.2.cloned.1.call-start = ((), (), s32[]{:S(2)}) async-start(), calls=%async_computation.4 | async-start | bytes 1048576 | tf_op jit(solution)/shard_map/psum | solution.py:34
  78.1 23.3 %copy-start.2 = (bf16[64,32,128]{2,1,0:T(8,128)(2,1)S(1)}, bf16[64,32,128]{2,1,0:T(8,128)(2,1)}, u32[]{:S(2)}) copy-start(bf16[64,32,128]{2,1,0:T(8,128)(2,1)} %param.9) | copy-start | bytes 1572868
  78.1 23.5 %copy-start.3 = (f32[128]{0:T(128)S(1)}, f32[128]{0:T(128)}, u32[]{:S(2)}) copy-start(f32[128]{0:T(128)} %param.8) | copy-start | bytes 1540
  101.4 4.5 %copy-start.1 = (bf16[2048,1024]{1,0:T(8,128)(2,1)S(1)}, bf16[2048,1024]{1,0:T(8,128)(2,1)}, u32[]{:S(2)}) copy-start(bf16[2048,1024]{1,0:T(8,128)(2,1)} %reshape.36) | copy-start | bytes 12582916
  108.1 131.0 %reduce-scatter.5.cloned.1.call-start = ((), (), s32[]{:S(2)}) async-start(), calls=%async_computation.3 | async-start | bytes 655360 | tf_op jit(solution)/shard_map/reduce_scatter | solution.py:47
  143.2 95.9 %reduce-scatter.3.cloned.1.call-start = ((), (), s32[]{:S(2)}) async-start(), calls=%async_computation.2 | async-start | bytes 1179648 | tf_op jit(solution)/shard_map/reduce_scatter | solution.py:44
Sparse Core Ops, SparseCore 0:
  108.2 130.8 all-reduce.1
Sparse Core Ops, SparseCore 1:
  143.3 22.7 reduce-scatter.4
  169.9 64.3 reduce-scatter.2
where the time goes:
time: 250 us; the launch traced here: 248 us
  waiting for transfers between devices  85.4 us (34%)
  local copies, waits for them, and re-layouts  72.9 us (29%)
  blocking collectives  39.4 us (16%)
  matrix products  34.8 us (14%)
  between operations  15.5 us (6%)
    psum x1, waiting for transfers between devices, shards(): proj_grad = lax.psum(weight_term, ('row', 'col'))  85.4 us
    all_gather x1, blocking collectives, shards(): left_all = lax.all_gather(left, 'col', axis=0, tiled=True)  33.4 us
    convert_element_type x1, local copies, waits for them, and re-layouts, shards(): outers = square.astype(jnp.bfloat16).reshape(rows_here * cols_here, OUTER)  24.6 us
    reshape x1, local copies, waits for them, and re-layouts, shards(): outers = square.astype(jnp.bfloat16).reshape(rows_here * cols_here, OUTER)  23.3 us
    reshape x1, local copies, waits for them, and re-layouts, shards(): grad_cube = grad_outer.reshape(rows_here, cols_here, CH, CH)  20.3 us
    dot_general x1, matrix products, shards(): jnp.einsum('ijce,sic->sje', grad_cube, left_cube, preferred_element_type=...  10.3 us
    dot_general x1, matrix products, shards(): jnp.einsum('ijce,sje->sic', grad_cube, right_cube, preferred_element_type...  9.14 us
    all_gather x1, blocking collectives, shards(): right_all = lax.all_gather(right, 'row', axis=0, tiled=True)  5.99 us
  transfers between devices with their start and end apart: 3, of which 1 were waited for; matrix products, arithmetic and copies ran while one was open for 18% of the time, Pallas kernels for 0%

commit v1 on v0

--- a/solution.py
+++ b/solution.py
@@ -9,8 +9,25 @@
 OUTER = 1024
 
 
+def joined_along(pieces, dim):
+    pieces = jnp.moveaxis(pieces, 0, dim)
+    shape = pieces.shape
+    return pieces.reshape(*shape[:dim], shape[dim] * shape[dim + 1], *shape[dim + 2 :])
+
+
+def grow_blocks(shard, axis):
+    size, mine = (lax.axis_size(axis), lax.axis_index(axis))
+    blocks, stride = (shard[None], 1)
+    while stride < size:
+        theirs = lax.ppermute(blocks, axis, [(i, i ^ stride) for i in range(size)])
+        low = mine & stride == 0
+        blocks = jnp.concatenate([jnp.where(low, blocks, theirs), jnp.where(low, theirs, blocks)])
+        stride *= 2
+    return blocks
+
+
 def shards(left, right, proj, bias, pair_grad):
-    left_all = lax.all_gather(left, "col", axis=0, tiled=True)
+    left_all = joined_along(grow_blocks(left, "col"), 0)
     right_all = lax.all_gather(right, "row", axis=0, tiled=True)
     seq_count = left_all.shape[0]
     rows_here = left_all.shape[1] // CH

time: 250 us -> 230 us (0.920)
  blocking collectives: 39.4 us -> 5.97 us
  local copies, waits for them, and re-layouts: 72.9 us -> 49.6 us
  waiting for transfers between devices: 85.4 us -> 99.7 us
  matrix products: 34.8 us -> 46.5 us
  starting transfers between devices: 0.31 us -> 8.2 us
  other arithmetic: 0.12 us -> 3.15 us
    all_gather x1 -> x0, blocking collectives: 33.4 us -> none  [shards(): left_all = lax.all_gather(left, 'col', axis=0, tiled=True)]
    convert_element_type x1 -> x0, local copies, waits for them, and re-layouts: 24.6 us -> none  [shards(): outers = square.astype(jnp.bfloat16).reshape(rows_here * cols_here, OUTER)]
    ppermute x0 -> x3, waiting for transfers between devices: none -> 12.7 us  [grow_blocks(): theirs = lax.ppermute(blocks, axis, [(i, i ^ stride) for i in range(size)])]
    dot_general x1, matrix products: 5.64 us -> 16.2 us  [shards(): jnp.einsum('sic,sje->ijce', left_cube, right_cube, preferred_element_type...]
    ppermute x0 -> x3, starting transfers between devices: none -> 7.86 us  [grow_blocks(): theirs = lax.ppermute(blocks, axis, [(i, i ^ stride) for i in range(size)])]
  transfers between devices with their start and end apart: 3 -> 6, of which waited for: 1 -> 3; matrix products, arithmetic and copies ran while one was open for 18% -> 20% of each run, Pallas kernels for 0% -> 0%
where the time goes in v1:
time: 230 us; the launch traced here: 229 us
  waiting for transfers between devices  99.7 us (43%)
  local copies, waits for them, and re-layouts  49.6 us (22%)
  matrix products  46.5 us (20%)
  between operations  15.6 us (7%)
  starting transfers between devices  8.2 us (4%)
  blocking collectives  5.97 us (3%)
  other arithmetic  3.15 us (1%)
    psum x1, waiting for transfers between devices, shards(): proj_grad = lax.psum(weight_term, ('row', 'col'))  87 us
    reshape x1, local copies, waits for them, and re-layouts, shards(): outers = square.astype(jnp.bfloat16).reshape(rows_here * cols_here, OUTER)  23.3 us
    reshape x1, local copies, waits for them, and re-layouts, shards(): grad_cube = grad_outer.reshape(rows_here, cols_here, CH, CH)  20.3 us
    dot_general x1, matrix products, shards(): jnp.einsum('sic,sje->ijce', left_cube, right_cube, preferred_element_type...  16.2 us
    ppermute x3, waiting for transfers between devices, grow_blocks(): theirs = lax.ppermute(blocks, axis, [(i, i ^ stride) for i in range(size)])  12.7 us
    dot_general x1, matrix products, shards(): jnp.einsum('ijce,sic->sje', grad_cube, left_cube, preferred_element_type=...  11 us
    dot_general x1, matrix products, shards(): jnp.einsum('ijce,sje->sic', grad_cube, right_cube, preferred_element_type...  9.24 us
    ppermute x3, starting transfers between devices, grow_blocks(): theirs = lax.ppermute(blocks, axis, [(i, i ^ stride) for i in range(size)])  7.86 us
  transfers between devices with their start and end apart: 6, of which 3 were waited for; matrix products, arithmetic and copies ran while one was open for 20% of the time, Pallas kernels for 0%

profile of v1, /device:TPU:0, one launch (start us, length us, event | category | flops | bytes accessed | tf_op | source)
XLA Modules:
  0.0 228.7 jit_solution(169458722630119557)
XLA Ops:
  8.0 0.0 copy-start
  8.0 0.0 all-reduce.2.cloned.1.call-start
  8.1 3.0 %collective-permute-start = (bf16[1,16,2048]{2,1,0:T(8,128)(2,1)}, bf16[1,16,2048]{2,1,0:T(8,128)(2,1)S(1)}, u32[]{:S(2)}, u32[]{:S(2)}) collective-permute-start(bf16[1,16,2048]{2,1,0:T(8,128)(2,1)} %bitcast.48), channel_id=1, source_target_pairs={{0,1},{1,0},{2,3},{3,2},{4,5},{5,4},{6,7},{7,6},{8,9},{9,8},{10,11... | collective-permute-start | bytes 196616 | tf_op jit(solution)/shard_map/ppermute | solution.py:22
  11.1 2.5 %collective-permute-done = bf16[1,16,2048]{2,1,0:T(8,128)(2,1)S(1)} collective-permute-done((bf16[1,16,2048]{2,1,0:T(8,128)(2,1)}, bf16[1,16,2048]{2,1,0:T(8,128)(2,1)S(1)}, u32[]{:S(2)}, u32[]{:S(2)}) %collective-permute-start) | collective-permute-done | bytes 65568 | tf_op jit(solution)/shard_map/ppermute | solution.py:22
  13.5 0.9 broadcast_select_fusion.5
  14.4 2.2 collective-permute-start.1
  16.6 6.0 %all_gather.3 = bf16[128,1024]{1,0:T(8,128)(2,1)S(1)} all-gather(bf16[32,1024]{1,0:T(8,128)(2,1)} %param.6), channel_id=1, replica_groups=mesh['row'=4,'col'=8] {'row'}, dimensions={0}, use_global_device_ids=true | all-gather | bytes 327680 | tf_op jit(solution)/shard_map/all_gather | solution.py:31
  22.6 0.2 copy.17
  22.7 0.0 collective-permute-done.1
  22.8 2.7 %collective-permute-start.2 = (bf16[4,16,2048]{2,1,0:T(8,128)(2,1)S(1)}, bf16[4,16,2048]{2,1,0:T(8,128)(2,1)S(1)}, u32[]{:S(2)}, u32[]{:S(2)}) collective-permute-start(bf16[4,16,2048]{2,1,0:T(8,128)(2,1)S(1)} %pad_maximum_fusion.1), channel_id=1, source_target_pairs={{0,4},{1,5},{2,6},{3,7},{4,0},{5,1},{6,2},{7,3},{8,12},{9,13},{10,... | collective-permute-start | bytes 786440 | tf_op jit(solution)/shard_map/ppermute | solution.py:22
  25.5 2.1 convert_multiply_fusion
  27.6 10.2 %collective-permute-done.2 = bf16[4,16,2048]{2,1,0:T(8,128)(2,1)S(1)} collective-permute-done((bf16[4,16,2048]{2,1,0:T(8,128)(2,1)S(1)}, bf16[4,16,2048]{2,1,0:T(8,128)(2,1)S(1)}, u32[]{:S(2)}, u32[]{:S(2)}) %collective-permute-start.2) | collective-permute-done | bytes 262176 | tf_op jit(solution)/shard_map/ppermute | solution.py:22
  37.9 1.6 reshape_reshape.3
  39.6 16.2 %fusion = bf16[64,32,32,32]{3,2,1,0:T(8,128)(2,1)} fusion(bf16[128,32,32,1]{0,2,1,3:T(8,128)(2,1)S(1)} %bitcast.43, bf16[128,64,32,1]{2,1,0,3:T(8,128)(2,1)S(1)} %bitcast.41), kind=kOutput, calls=%fused_computation.1 | convolution fusion | flops 541065216 | bytes 4980736 | tf_op jit(solution)/shard_map/sic,sje->ijce/dot_general | solution.py:38
  55.8 0.0 copy-start.2
  55.8 23.3 %reshape.32 = bf16[2048,1024]{1,0:T(8,128)(2,1)} reshape(bf16[64,32,32,32]{3,2,1,0:T(8,128)(2,1)} %fusion) | data formatting | bytes 8388608 | tf_op jit(solution)/shard_map/reshape | solution.py:41
  79.1 0.0 copy-done
  79.1 0.0 copy-done.2
  79.1 0.0 copy-start.1
  79.1 4.7 %fusion.17 = (bf16[2048,128]{1,0:T(8,128)(2,1)S(1)}, bf16[2048,128]{1,0:T(8,128)(2,1)}) fusion(f32[64,32,128]{2,1,0:T(8,128)} %convert_multiply_fusion, f32[128]{0:T(128)S(1)} %copy-done.2, bf16[2048,1024]{1,0:T(8,128)(2,1)} %reshape.32, bf16[1024,128]{1,0:T(8,128)(2,1)S(1)} %copy-done), kind=kOutput, calls=%fused_computation.14 | convolution fusion | flops 538443776 | bytes 6554112 | tf_op jit(solution)/shard_map/dot_general | solution.py:42
  83.8 0.0 copy-done.1
  83.8 2.1 fusion.18
  85.9 3.2 %convolution_convert_fusion = bf16[2048,1024]{1,0:T(8,128)(2,1)} fusion(bf16[2048,128]{1,0:T(8,128)(2,1)S(1)} %get-tuple-element.4, bf16[1024,128]{1,0:T(8,128)(2,1)S(1)} %copy-done), kind=kOutput, calls=%fused_computation.4 | convolution fusion | flops 538968064 | bytes 4980736 | tf_op jit(solution)/shard_map/dot_general | solution.py:52
  89.1 0.0 all-reduce.2.cloned.1.call-update
  89.1 0.0 reduce-scatter.5.cloned.1.call-start
  89.1 20.3 %reshape.34 = bf16[64,32,32,32]{3,2,1,0:T(8,128)(2,1)} reshape(bf16[2048,1024]{1,0:T(8,128)(2,1)} %convolution_convert_fusion) | data formatting | bytes 8388608 | tf_op jit(solution)/shard_map/reshape | solution.py:53
  109.5 11.0 %fusion.12 = f32[128,32,32]{0,2,1:T(8,128)S(1)} fusion(bf16[64,32,32,32]{3,2,1,0:T(8,128)(2,1)} %reshape.34, bf16[128,64,32,1]{2,1,0,3:T(8,128)(2,1)S(1)} %bitcast.42), kind=kOutput, calls=%fused_computation.12 | convolution fusion | flops 537001984 | bytes 5242880 | tf_op jit(solution)/shard_map/ijce,sic->sje/dot_general | solution.py:59
  120.5 1.0 copy.24
  121.5 0.0 reduce-scatter.5.cloned.1.call-update
  121.5 0.3 reduce-scatter.3.cloned.1.call-start
  121.8 9.2 %fusion.6 = f32[64,32,128]{2,1,0:T(8,128)S(1)} fusion(bf16[64,32,32,32]{3,2,1,0:T(8,128)(2,1)} %reshape.34, bf16[128,32,32,1]{0,2,1,3:T(8,128)(2,1)S(1)} %bitcast.44), kind=kOutput, calls=%fused_computation.10 | convolution fusion | flops 537133056 | bytes 5505024 | tf_op jit(solution)/shard_map/ijce,sje->sic/dot_general | solution.py:55
  131.1 1.3 copy.21
  132.4 0.0 reduce-scatter.3.cloned.1.call-update
  132.4 87.0 %all-reduce.2.cloned.1.call-done = f32[1024,128]{1,0:T(8,128)} async-done(((f32[1024,128]{1,0:T(8,128)}), f32[1024,128]{1,0:T(8,128)}) %all-reduce.2.cloned.1.call-update) | async-done | bytes 524304 | tf_op jit(solution)/shard_map/psum | solution.py:51
  219.4 0.0 reduce-scatter.5.cloned.1.call-done
  219.4 0.0 reduce-scatter.3.cloned.1.call-done
  219.4 1.9 copy.53
  (5 shorter events, 0.2 us)
Async XLA Ops:
  8.0 71.1 %copy-start = (bf16[1024,128]{1,0:T(8,128)(2,1)S(1)}, bf16[1024,128]{1,0:T(8,128)(2,1)}, u32[]{:S(2)}) copy-start(bf16[1024,128]{1,0:T(8,128)(2,1)} %param.7) | copy-start | bytes 786436
  8.0 211.4 %all-reduce.2.cloned.1.call-start = ((), (), s32[]{:S(2)}) async-start(), calls=%async_computation.4 | async-start | bytes 1048576 | tf_op jit(solution)/shard_map/psum | solution.py:51
  8.1 5.5 %collective-permute-start = (bf16[1,16,2048]{2,1,0:T(8,128)(2,1)}, bf16[1,16,2048]{2,1,0:T(8,128)(2,1)S(1)}, u32[]{:S(2)}, u32[]{:S(2)}) collective-permute-start(bf16[1,16,2048]{2,1,0:T(8,128)(2,1)} %bitcast.48), channel_id=1, source_target_pairs={{0,1},{1,0},{2,3},{3,2},{4,5},{5,4},{6,7},{7,6},{8,9},{9,8},{10,11... | collective-permute-start | bytes 196616 | tf_op jit(solution)/shard_map/ppermute | solution.py:22
  14.4 8.3 %collective-permute-start.1 = (bf16[2,16,2048]{2,1,0:T(8,128)(2,1)S(1)}, bf16[2,16,2048]{2,1,0:T(8,128)(2,1)S(1)}, u32[]{:S(2)}, u32[]{:S(2)}) collective-permute-start(bf16[2,16,2048]{2,1,0:T(8,128)(2,1)S(1)} %pad_maximum_fusion.2), channel_id=1, source_target_pairs={{0,2},{1,3},{2,0},{3,1},{4,6},{5,7},{6,4},{7,5},{8,10},{9,11},{10,... | collective-permute-start | bytes 393224 | tf_op jit(solution)/shard_map/ppermute | solution.py:22
  22.8 15.0 %collective-permute-start.2 = (bf16[4,16,2048]{2,1,0:T(8,128)(2,1)S(1)}, bf16[4,16,2048]{2,1,0:T(8,128)(2,1)S(1)}, u32[]{:S(2)}, u32[]{:S(2)}) collective-permute-start(bf16[4,16,2048]{2,1,0:T(8,128)(2,1)S(1)} %pad_maximum_fusion.1), channel_id=1, source_target_pairs={{0,4},{1,5},{2,6},{3,7},{4,0},{5,1},{6,2},{7,3},{8,12},{9,13},{10,... | collective-permute-start | bytes 786440 | tf_op jit(solution)/shard_map/ppermute | solution.py:22
  55.8 23.3 %copy-start.2 = (f32[128]{0:T(128)S(1)}, f32[128]{0:T(128)}, u32[]{:S(2)}) copy-start(f32[128]{0:T(128)} %param.8) | copy-start | bytes 1540
  79.1 4.7 %copy-start.1 = (bf16[2048,1024]{1,0:T(8,128)(2,1)S(1)}, bf16[2048,1024]{1,0:T(8,128)(2,1)}, u32[]{:S(2)}) copy-start(bf16[2048,1024]{1,0:T(8,128)(2,1)} %reshape.32) | copy-start | bytes 12582916
  89.1 130.3 %reduce-scatter.5.cloned.1.call-start = ((), (), s32[]{:S(2)}) async-start(), calls=%async_computation.3 | async-start | bytes 655360 | tf_op jit(solution)/shard_map/reduce_scatter | solution.py:64
  121.5 97.9 %reduce-scatter.3.cloned.1.call-start = ((), (), s32[]{:S(2)}) async-start(), calls=%async_computation.2 | async-start | bytes 1179648 | tf_op jit(solution)/shard_map/reduce_scatter | solution.py:61
Sparse Core Ops, SparseCore 0:
  89.2 130.1 all-reduce.1
Sparse Core Ops, SparseCore 1:
  121.6 21.9 reduce-scatter.4
  147.4 64.3 reduce-scatter.2
